TPU v7x, 32 devices: a whole 2x2x4 slice. The times are simulated.
32 devices in a mesh: row: 4 (over z), col: 8 (over y, x, core).
Axes of the slice: x: 2, y: 2, z: 4, core: 2. Of those that a mesh axis runs over, the one named last changes fastest.
Arguments:
- trailing: float32 [16384, 16384], P('row', 'col'), may hold values from -51 to 51
- panel_cols: float32 [16384, 128], P(('row', 'col')), as said below
Outputs:
- updated: float32 [16384, 16384], P('row', 'col')
- triangle: float32 [128, 128], replicated
Inputs may be any that keep to these rules, and one draw needn't show every extreme that they name: panel_cols has full column rank.
All inputs are finite; a program needn't handle non-finite values.
Results may differ from a plain program's by a relative error of at most 0.00005.
Values sent between devices are 32-bit elements; how exact they have to be, the bound alone decides.
No kernel may reach another device: no remote copies, remote signals or barrier semaphores. Data moves between devices by JAX's collectives and lax.ppermute only.
A program may use at most 128 MiB of HBM per device.

v0:
```python
import jax
import jax.numpy as jnp
from jax import lax
from jax.sharding import PartitionSpec as P


def spread(array, axis, root):
    mine = lax.axis_index(axis) == root
    return lax.psum(jnp.where(mine, array, jnp.zeros_like(array)), axis)


def matmul(left_side, right_side):
    return jnp.dot(
        left_side, right_side, precision=lax.Precision.HIGHEST, preferred_element_type=jnp.float32
    )


def local(trailing, panel_cols):
    rows_here = trailing.shape[0]
    cols_here = trailing.shape[1]
    blocks_per = rows_here // cols_here
    row_index = lax.axis_index("row")
    col_index = lax.axis_index("col")
    gram_sum = lax.psum(matmul(panel_cols.T, panel_cols), ("row", "col"))
    factor = jnp.linalg.cholesky(gram_sum)
    basis_own = lax.linalg.triangular_solve(factor, panel_cols.T, left_side=True, lower=True).T
    basis_all = lax.all_gather(basis_own, ("row", "col"), axis=0, tiled=True)
    basis_rows = lax.dynamic_slice_in_dim(basis_all, row_index * rows_here, rows_here, 0)
    basis_cols = lax.dynamic_slice_in_dim(basis_all, col_index * cols_here, cols_here, 0)
    partial_value = matmul(trailing, basis_cols)
    image_rows = lax.psum(partial_value, "col")
    coupling = lax.psum(matmul(basis_rows.T, image_rows), "row")
    shift_rows = 2.0 * image_rows - 2.0 * matmul(basis_rows, coupling)
    shift_part = lax.dynamic_slice_in_dim(
        shift_rows, col_index % blocks_per * cols_here, cols_here, 0
    )
    shift_cols = spread(shift_part, "row", col_index // blocks_per)
    left_side = jnp.concatenate([basis_rows, shift_rows], axis=1)
    right_side = jnp.concatenate([shift_cols, basis_cols], axis=1)
    updated = trailing - matmul(left_side, right_side.T)
    return (updated, factor.T)


def solution(mesh):
    in_specs = (P("row", "col"), P(("row", "col"), None))
    out_specs = (P("row", "col"), P())
    return jax.shard_map(local, mesh=mesh, in_specs=in_specs, out_specs=out_specs, check_vma=False)
```

profile of v0, /device:TPU:0, one launch (start us, length us, event | category | flops | bytes accessed | tf_op | source)
XLA Modules:
  0.0 478.7 jit_solution(13148637477328393549)
XLA Ops:
  7.2 0.0 copy-start
  7.2 0.0 all-reduce.5.cloned.1.call-start
  7.2 0.9 copy-done
  8.1 1.2 fusion.11
  9.3 0.0 all-reduce.5.cloned.1.call-update
  9.4 0.0 all-gather.2.cloned.1.call-start
  9.4 126.9 %all-reduce.5.cloned.1.call-done = f32[128,128]{0,1:T(8,128)} async-done(((f32[128,128]{0,1:T(8,128)}), f32[128,128]{0,1:T(8,128)}) %all-reduce.5.cloned.1.call-update) | async-done | bytes 65552 | tf_op jit(solution)/shard_map/psum | solution.py:24
  136.3 0.9 copy.5
  137.2 0.9 fusion.8
  138.1 11.7 %cholesky.16 = f32[128,128]{1,0:T(8,128)S(1)} custom-call(f32[128,128]{1,0:T(8,128)S(1)} %fusion.8), custom_call_target="Cholesky" | custom-call | tf_op jit(solution)/shard_map/jit(cholesky)/cholesky | solution.py:25
  149.8 0.6 compare_reduce_fusion
  150.5 0.7 fusion.9
  151.1 9.8 %custom-call.6 = f32[1,128,128]{1,2,0:T(8,128)S(1)} custom-call(f32[1,128,128]{2,1,0:T(8,128)S(1)} %get-tuple-element.5), custom_call_target="InvertDiagBlocksLowerTriangular" | custom-call | tf_op jit(solution)/shard_map/triangular_solve | solution.py:26
  160.9 1.1 convolution_bitcast_fusion.1
  162.1 0.0 all-gather.2.cloned.1.call-update
  162.1 0.2 all-reduce.7.cloned.1.call-start
  162.3 78.6 %all-gather.2.cloned.1.call-done = f32[16384,128]{0,1:T(8,128)} async-done(((f32[512,128]{0,1:T(8,128)}), f32[16384,128]{0,1:T(8,128)}) %all-gather.2.cloned.1.call-update) | async-done | bytes 8388624 | tf_op jit(solution)/shard_map/all_gather | solution.py:27
  240.9 1.3 constant_dynamic-slice_fusion
  242.2 38.6 %convolution_bitcast_fusion = f32[4096,128]{0,1:T(8,128)} fusion(f32[2048,128]{0,1:T(8,128)S(1)} %constant_dynamic-slice_fusion, f32[4096,2048]{1,0:T(8,128)} %param.2), kind=kOutput, calls=%fused_computation.3 | convolution fusion | flops 12884901888 | bytes 36700160 | tf_op jit(solution)/shard_map/dot_general | solution.py:13
  280.8 0.0 all-reduce.7.cloned.1.call-update
  280.8 0.0 all-reduce.9.cloned.1.call-start
  280.9 1.7 constant_dynamic-slice_fusion.1
  282.7 59.4 %all-reduce.7.cloned.1.call-done = f32[4096,128]{0,1:T(8,128)} async-done(((f32[4096,128]{0,1:T(8,128)}), f32[4096,128]{0,1:T(8,128)}) %all-reduce.7.cloned.1.call-update) | async-done | bytes 2097168 | tf_op jit(solution)/shard_map/psum | solution.py:31
  342.0 4.1 fusion.12
  346.1 0.0 all-reduce.9.cloned.1.call-update
  346.1 0.3 all-reduce.11.cloned.1.call-start
  346.4 33.2 %all-reduce.9.cloned.1.call-done = f32[128,128]{1,0:T(8,128)} async-done(((f32[128,128]{1,0:T(8,128)}), f32[128,128]{1,0:T(8,128)}) %all-reduce.9.cloned.1.call-update) | async-done | bytes 65552 | tf_op jit(solution)/shard_map/psum | solution.py:32
  379.6 3.8 fusion
  383.4 0.0 copy-start.2
  383.4 1.3 copy-done.2
  384.8 1.0 dynamic-slice_select_fusion
  385.8 0.0 all-reduce.11.cloned.1.call-update
  385.8 0.7 copy.6
  386.6 51.0 %all-reduce.11.cloned.1.call-done = f32[2048,128]{0,1:T(8,128)} async-done(((f32[2048,128]{0,1:T(8,128)}), f32[2048,128]{0,1:T(8,128)}) %all-reduce.11.cloned.1.call-update) | async-done | bytes 1048592 | tf_op jit(solution)/shard_map/psum | solution.py:9
  437.6 0.0 copy-start.1
  437.6 34.6 %convolution_subtract_fusion = f32[4096,2048]{1,0:T(8,128)} fusion(f32[4096,2048]{1,0:T(8,128)} %param.2, f32[4096,128]{0,1:T(8,128)} %copy-done.2, f32[4096,128]{0,1:T(8,128)S(1)} %constant_dynamic-slice_fusion.1, f32[2048,128]{0,1:T(8,128)S(1)} %constant_dynamic-slice_fusion, f32[2048,128]{0,1:T(8,128)} %all-reduce.11.cloned.1.call-done), kind=kOutput, calls=%fused_computation | convolution fusion | flops 25779765248 | bytes 73400320 | tf_op jit(solution)/shard_map/dot_general | solution.py:13
  472.1 0.0 copy-done.1
  (1 shorter events, 0.0 us)
Async XLA Ops:
  7.2 1.0 copy-start
  7.2 129.1 %all-reduce.5.cloned.1.call-start = ((), (), s32[]{:S(2)}) async-start(), calls=%async_computation | async-start | bytes 131072 | tf_op jit(solution)/shard_map/psum | solution.py:24
  9.4 231.6 %all-gather.2.cloned.1.call-start = ((), (), s32[]{:S(2)}) async-start(), calls=%async_computation.1 | async-start | bytes 8650752 | tf_op jit(solution)/shard_map/all_gather | solution.py:27
  162.1 179.9 %all-reduce.7.cloned.1.call-start = ((), (), s32[]{:S(2)}) async-start(), calls=%async_computation.2 | async-start | bytes 4194304 | tf_op jit(solution)/shard_map/psum | solution.py:31
  280.8 98.8 %all-reduce.9.cloned.1.call-start = ((), (), s32[]{:S(2)}) async-start(), calls=%async_computation.3 | async-start | bytes 131072 | tf_op jit(solution)/shard_map/psum | solution.py:32
  346.1 91.5 %all-reduce.11.cloned.1.call-start = ((), (), s32[]{:S(2)}) async-start(), calls=%async_computation.4 | async-start | bytes 2097152 | tf_op jit(solution)/shard_map/psum | solution.py:9
  383.4 1.3 copy-start.2
  437.6 34.6 %copy-start.1 = (f32[512,128]{1,0:T(8,128)S(1)}, f32[512,128]{1,0:T(8,128)}, u32[]{:S(2)}) copy-start(f32[512,128]{1,0:T(8,128)} %param.3) | copy-start | bytes 786436
Sparse Core Ops, SparseCore 0:
  14.1 122.0 all-reduce.4
  162.2 78.6 all-gather.1
  281.0 60.9 all-reduce.6
  346.2 33.3 all-reduce.8
  386.0 51.5 all-reduce.10
where the time goes:
time: 479 us
  waiting for transfers between devices  349 us (73%)
  matrix products  83.4 us (17%)
  other arithmetic  24.8 us (5%)
  between operations  13.9 us (3%)
  local copies, waits for them, and re-layouts  6.96 us (1%)
    psum x1, waiting for transfers between devices, local(): gram_sum = lax.psum(matmul(panel_cols.T, panel_cols), ('row', 'col'))  127 us
    dot_general x5, matrix products, matmul(): jnp.dot(left_side, right_side, precision=lax.Precision.HIGHEST, preferred...  82.2 us
    all_gather x1, waiting for transfers between devices, local(): basis_all = lax.all_gather(basis_own, ('row', 'col'), axis=0, tiled=True)  78.6 us
    psum x1, waiting for transfers between devices, local(): image_rows = lax.psum(partial_value, 'col')  59.4 us
    psum x1, waiting for transfers between devices, spread(): return lax.psum(jnp.where(mine, array, jnp.zeros_like(array)), axis)  51 us
    psum x1, waiting for transfers between devices, local(): coupling = lax.psum(matmul(basis_rows.T, image_rows), 'row')  33.2 us
    another operation x3, other arithmetic, local(): factor = jnp.linalg.cholesky(gram_sum)  12.4 us
    another operation x1, other arithmetic, local(): lax.linalg.triangular_solve(factor, panel_cols.T, left_side=True, lower=T...  9.81 us
  transfers between devices with their start and end apart: 5, of which 5 were waited for; matrix products, arithmetic and copies ran while one was open for 1% of the time, Pallas kernels for 0%

commit v1 on v0

--- a/solution.py
+++ b/solution.py
@@ -29,7 +29,7 @@
     basis_cols = lax.dynamic_slice_in_dim(basis_all, col_index * cols_here, cols_here, 0)
     partial_value = matmul(trailing, basis_cols)
     image_rows = lax.psum(partial_value, "col")
-    coupling = lax.psum(matmul(basis_rows.T, image_rows), "row")
+    coupling = jnp.sum(lax.all_gather(matmul(basis_rows.T, image_rows), "row"), axis=0)
     shift_rows = 2.0 * image_rows - 2.0 * matmul(basis_rows, coupling)
     shift_part = lax.dynamic_slice_in_dim(
         shift_rows, col_index % blocks_per * cols_here, cols_here, 0

time: 479 us -> 459 us (0.958)
  waiting for transfers between devices: 349 us -> 316 us
  blocking collectives: 0 us -> 14.2 us
    psum x1 -> x0, waiting for transfers between devices: 33.2 us -> none  [local(): coupling = lax.psum(matmul(basis_rows.T, image_rows), 'row')]
    all_gather x0 -> x1, blocking collectives: none -> 14.2 us  [local(): lax.all_gather(matmul(basis_rows.T, image_rows), 'row')]
  transfers between devices with their start and end apart: 5 -> 4, of which waited for: 5 -> 4; matrix products, arithmetic and copies ran while one was open for 1% -> 1% of each run, Pallas kernels for 0% -> 0%
where the time goes in v1:
time: 459 us
  waiting for transfers between devices  316 us (69%)
  matrix products  82.7 us (18%)
  other arithmetic  24.8 us (5%)
  blocking collectives  14.2 us (3%)
  between operations  13.9 us (3%)
  local copies, waits for them, and re-layouts  6.97 us (2%)
    psum x1, waiting for transfers between devices, local(): gram_sum = lax.psum(matmul(panel_cols.T, panel_cols), ('row', 'col'))  127 us
    dot_general x5, matrix products, matmul(): jnp.dot(left_side, right_side, precision=lax.Precision.HIGHEST, preferred...  81.5 us
    all_gather x1, waiting for transfers between devices, local(): basis_all = lax.all_gather(basis_own, ('row', 'col'), axis=0, tiled=True)  78.6 us
    psum x1, waiting for transfers between devices, local(): image_rows = lax.psum(partial_value, 'col')  59.4 us
    psum x1, waiting for transfers between devices, spread(): return lax.psum(jnp.where(mine, array, jnp.zeros_like(array)), axis)  51 us
    all_gather x1, blocking collectives, local(): lax.all_gather(matmul(basis_rows.T, image_rows), 'row')  14.2 us
    another operation x3, other arithmetic, local(): factor = jnp.linalg.cholesky(gram_sum)  12.4 us
    another operation x1, other arithmetic, local(): lax.linalg.triangular_solve(factor, panel_cols.T, left_side=True, lower=T...  9.81 us
  transfers between devices with their start and end apart: 4, of which 4 were waited for; matrix products, arithmetic and copies ran while one was open for 1% of the time, Pallas kernels for 0%

profile of v1, /device:TPU:0, one launch (start us, length us, event | category | flops | bytes accessed | tf_op | source)
XLA Modules:
  0.0 458.7 jit_solution(82577340016183719)
XLA Ops:
  7.2 0.0 copy-start
  7.2 0.0 all-reduce.4.cloned.1.call-start
  7.2 0.9 copy-done
  8.1 1.2 fusion.11
  9.3 0.0 all-reduce.4.cloned.1.call-update
  9.4 0.0 all-gather.3.cloned.1.call-start
  9.4 126.9 %all-reduce.4.cloned.1.call-done = f32[128,128]{0,1:T(8,128)} async-done(((f32[128,128]{0,1:T(8,128)}), f32[128,128]{0,1:T(8,128)}) %all-reduce.4.cloned.1.call-update) | async-done | bytes 65552 | tf_op jit(solution)/shard_map/psum | solution.py:24
  136.3 0.9 copy.5
  137.2 0.9 fusion.8
  138.1 11.7 %cholesky.16 = f32[128,128]{1,0:T(8,128)S(1)} custom-call(f32[128,128]{1,0:T(8,128)S(1)} %fusion.8), custom_call_target="Cholesky" | custom-call | tf_op jit(solution)/shard_map/jit(cholesky)/cholesky | solution.py:25
  149.8 0.6 compare_reduce_fusion
  150.5 0.7 fusion.9
  151.1 9.8 %custom-call.6 = f32[1,128,128]{1,2,0:T(8,128)S(1)} custom-call(f32[1,128,128]{2,1,0:T(8,128)S(1)} %get-tuple-element.5), custom_call_target="InvertDiagBlocksLowerTriangular" | custom-call | tf_op jit(solution)/shard_map/triangular_solve | solution.py:26
  160.9 1.1 convolution_bitcast_fusion.1
  162.1 0.0 all-gather.3.cloned.1.call-update
  162.1 0.2 all-reduce.6.cloned.1.call-start
  162.3 78.6 %all-gather.3.cloned.1.call-done = f32[16384,128]{0,1:T(8,128)} async-done(((f32[512,128]{0,1:T(8,128)}), f32[16384,128]{0,1:T(8,128)}) %all-gather.3.cloned.1.call-update) | async-done | bytes 8388624 | tf_op jit(solution)/shard_map/all_gather | solution.py:27
  240.9 1.3 constant_dynamic-slice_fusion
  242.3 38.6 %convolution_bitcast_fusion = f32[4096,128]{0,1:T(8,128)} fusion(f32[2048,128]{0,1:T(8,128)S(1)} %constant_dynamic-slice_fusion, f32[4096,2048]{1,0:T(8,128)} %param.2), kind=kOutput, calls=%fused_computation.3 | convolution fusion | flops 12884901888 | bytes 36700160 | tf_op jit(solution)/shard_map/dot_general | solution.py:13
  280.8 0.0 all-reduce.6.cloned.1.call-update
  280.9 0.0 all-reduce.8.cloned.1.call-start
  280.9 1.7 constant_dynamic-slice_fusion.1
  282.7 59.4 %all-reduce.6.cloned.1.call-done = f32[4096,128]{0,1:T(8,128)} async-done(((f32[4096,128]{0,1:T(8,128)}), f32[4096,128]{0,1:T(8,128)}) %all-reduce.6.cloned.1.call-update) | async-done | bytes 2097168 | tf_op jit(solution)/shard_map/psum | solution.py:31
  342.0 3.4 fusion.12
  345.5 14.2 %all-gather = f32[512,128]{1,0:T(8,128)S(1)} all-gather(f32[128,128]{1,0:T(8,128)S(1)} %fusion.12), channel_id=2, replica_groups=mesh['row'=4,'col'=8] {'row'}, dimensions={0}, use_global_device_ids=true | all-gather | bytes 327680 | tf_op jit(solution)/shard_map/all_gather | solution.py:32
  359.6 3.8 fusion
  363.4 0.0 copy-start.2
  363.4 1.3 copy-done.2
  364.8 1.0 dynamic-slice_select_fusion
  365.8 0.0 all-reduce.8.cloned.1.call-update
  365.8 0.7 copy.6
  366.6 51.0 %all-reduce.8.cloned.1.call-done = f32[2048,128]{0,1:T(8,128)} async-done(((f32[2048,128]{0,1:T(8,128)}), f32[2048,128]{0,1:T(8,128)}) %all-reduce.8.cloned.1.call-update) | async-done | bytes 1048592 | tf_op jit(solution)/shard_map/psum | solution.py:9
  417.6 0.0 copy-start.1
  417.6 34.6 %convolution_subtract_fusion = f32[4096,2048]{1,0:T(8,128)} fusion(f32[4096,2048]{1,0:T(8,128)} %param.2, f32[4096,128]{0,1:T(8,128)} %copy-done.2, f32[4096,128]{0,1:T(8,128)S(1)} %constant_dynamic-slice_fusion.1, f32[2048,128]{0,1:T(8,128)S(1)} %constant_dynamic-slice_fusion, f32[2048,128]{0,1:T(8,128)} %all-reduce.8.cloned.1.call-done), kind=kOutput, calls=%fused_computation | convolution fusion | flops 25779765248 | bytes 73400320 | tf_op jit(solution)/shard_map/dot_general | solution.py:13
  452.1 0.0 copy-done.1
  (2 shorter events, 0.1 us)
Async XLA Ops:
  7.2 1.0 copy-start
  7.2 129.1 %all-reduce.4.cloned.1.call-start = ((), (), s32[]{:S(2)}) async-start(), calls=%async_computation | async-start | bytes 131072 | tf_op jit(solution)/shard_map/psum | solution.py:24
  9.4 231.6 %all-gather.3.cloned.1.call-start = ((), (), s32[]{:S(2)}) async-start(), calls=%async_computation.1 | async-start | bytes 8650752 | tf_op jit(solution)/shard_map/all_gather | solution.py:27
  162.1 179.9 %all-reduce.6.cloned.1.call-start = ((), (), s32[]{:S(2)}) async-start(), calls=%async_computation.2 | async-start | bytes 4194304 | tf_op jit(solution)/shard_map/psum | solution.py:31
  280.9 136.7 %all-reduce.8.cloned.1.call-start = ((), (), s32[]{:S(2)}) async-start(), calls=%async_computation.3 | async-start | bytes 2097152 | tf_op jit(solution)/shard_map/psum | solution.py:9
  363.4 1.4 copy-start.2
  417.6 34.6 %copy-start.1 = (f32[512,128]{1,0:T(8,128)S(1)}, f32[512,128]{1,0:T(8,128)}, u32[]{:S(2)}) copy-start(f32[512,128]{1,0:T(8,128)} %param.3) | copy-start | bytes 786436
Sparse Core Ops, SparseCore 0:
  14.1 122.0 all-reduce.3
  162.2 78.6 all-gather.2
  281.0 61.0 all-reduce.5
  366.0 51.5 all-reduce.7
